TPU v7x, 32 devices: a whole 2x2x4 slice. The times are simulated.
32 devices in a mesh: rep: 2 (over x), blk: 16 (over z, y, core).
Axes of the slice: x: 2, y: 2, z: 4, core: 2. Of those that a mesh axis runs over, the one named last changes fastest.
Arguments:
- features: bfloat16 [4096, 512], P(('rep', 'blk')), may hold values from -6 to 6
- weight: bfloat16 [512, 512], replicated, may hold values from -0.25 to 0.25
- tile_values: bfloat16 [2, 16, 16, 2, 128, 128], P('rep', 'blk'), as said below
- tile_list: int32 [2, 16, 16, 2], P('rep', 'blk'), may hold values from -1 to 1, as said below
- train_mask: int32 [4096], P(('rep', 'blk')), may hold values 0 or 1
- cotangent: bfloat16 [4096, 512], P(('rep', 'blk')), may hold values from -6 to 6
Outputs:
- activated: bfloat16 [4096, 512], P(('rep', 'blk'))
- weight_grad: float32 [512, 512], replicated
- feature_grad: bfloat16 [4096, 512], P(('rep', 'blk'))
Inputs may be any that keep to these rules, and one draw needn't show every extreme that they name: `tile_list`: -1 marks an empty slot; 0 or 1 names the half h whose tile [r, b, j, h] is nonempty; the two slots of a pair never name the same half. The graph is undirected: block (u, v) of A is nonempty exactly when block (v, u) is, and every block (u, u) is nonempty. How many nonempty tiles a device holds differs from device to device. `tile_values`: the tile of block (u, v) is the transpose of the tile of block (v, u), so A is symmetric.
All inputs are finite; a program needn't handle non-finite values. No bound on the sum of `train_mask` on one device may be relied on, other than what follows from the above.
Results may differ from a plain program's by a relative error of at most 0.014.
Values may be sent and summed in bfloat16 or wider, within the bound.
A program may use at most 128 MiB of HBM per device.

v0:
```python
import math

import jax
import jax.numpy as jnp
from jax import lax
from jax.sharding import PartitionSpec as P

GELU_SCALE = math.sqrt(2.0 / math.pi)


def activation(pre_act):
    inner = GELU_SCALE * (pre_act + 0.044715 * pre_act * pre_act * pre_act)
    tanh_part = jnp.tanh(inner)
    act_value = 0.5 * pre_act * (1.0 + tanh_part)
    act_slope = 0.5 * (1.0 + tanh_part) + 0.5 * pre_act * (
        1.0 - tanh_part * tanh_part
    ) * GELU_SCALE * (1.0 + 3.0 * 0.044715 * pre_act * pre_act)
    return (act_value, act_slope)


def on_device(features, weight, tile_values, tile_list, train_mask, cotangent):
    tile_rows = features.shape[0]
    feat_width = features.shape[1]
    pair_list = tile_list[0, 0]
    presence = jnp.stack(
        [jnp.any(pair_list == 0, axis=1), jnp.any(pair_list == 1, axis=1)], axis=1
    ).astype(jnp.bfloat16)
    masked = tile_values[0, 0] * presence[:, :, None, None]
    projected = jnp.dot(features, weight, preferred_element_type=jnp.float32).astype(jnp.bfloat16)

    def apply_tiles(incoming):
        shard_count = incoming.shape[0] // tile_rows
        return jnp.einsum(
            "jhst,jtf->hsf",
            masked,
            incoming.reshape(shard_count, tile_rows, feat_width),
            preferred_element_type=jnp.float32,
        )

    partial_value = apply_tiles(lax.all_gather(projected, "blk", axis=0, tiled=True))
    summed = lax.psum_scatter(
        partial_value.reshape(2 * tile_rows, feat_width).astype(jnp.bfloat16),
        "rep",
        scatter_dimension=0,
        tiled=True,
    ).astype(jnp.float32)
    act_value, act_slope = activation(summed)
    activated = act_value.astype(jnp.bfloat16)
    grad_z = (
        cotangent.astype(jnp.float32) * train_mask.astype(jnp.float32)[:, None] * act_slope
    ).astype(jnp.bfloat16)
    folded = apply_tiles(lax.all_gather(grad_z, "blk", axis=0, tiled=True))
    prop_sums = lax.psum_scatter(
        folded.reshape(2 * tile_rows, feat_width).astype(jnp.bfloat16),
        "rep",
        scatter_dimension=0,
        tiled=True,
    )
    local_term = lax.dot_general(
        features, prop_sums, (((0,), (0,)), ((), ())), preferred_element_type=jnp.float32
    )
    weight_grad = lax.psum(local_term, ("rep", "blk"))
    feature_grad = lax.dot_general(
        prop_sums, weight, (((1,), (1,)), ((), ())), preferred_element_type=jnp.float32
    ).astype(jnp.bfloat16)
    return (activated, weight_grad, feature_grad)


def solution(mesh):
    in_specs = (
        P(("rep", "blk"), None),
        P(),
        P("rep", "blk", None, None, None, None),
        P("rep", "blk", None, None),
        P(("rep", "blk")),
        P(("rep", "blk"), None),
    )
    out_specs = (P(("rep", "blk"), None), P(), P(("rep", "blk"), None))
    return jax.shard_map(
        on_device, mesh=mesh, in_specs=in_specs, out_specs=out_specs, check_vma=False
    )
```

profile of v0, /device:TPU:1, one launch (start us, length us, event | category | flops | bytes accessed | tf_op | source)
XLA Modules:
  0.0 270.3 jit_solution(10915368503565097484)
XLA Ops:
  7.2 0.0 copy-start
  7.2 0.0 all-gather.3.cloned.1.call-start
  7.2 1.0 copy-done
  8.2 1.8 convolution_convert_fusion.1
  10.0 0.0 all-gather.3.cloned.1.call-update
  10.0 0.0 reduce-scatter.3.cloned.1.call-start
  10.1 0.7 compare_reduce_fusion.1
  10.8 0.1 copy.9
  10.9 1.4 bitcast_multiply_fusion
  12.3 0.0 copy-start.4
  12.3 0.0 copy-start.3
  12.3 42.4 %all-gather.3.cloned.1.call-done = bf16[2048,512]{1,0:T(8,128)(2,1)} async-done(((bf16[128,512]{1,0:T(8,128)(2,1)}), bf16[2048,512]{1,0:T(8,128)(2,1)}) %all-gather.3.cloned.1.call-update) | async-done | bytes 2097168 | tf_op jit(solution)/shard_map/all_gather | solution.py:40
  54.7 3.0 %fusion = bf16[256,512]{1,0:T(8,128)(2,1)} fusion(bf16[256,16,128]{2,0,1:T(8,128)(2,1)S(1)} %bitcast.29, bf16[16,128,512]{2,1,0:T(8,128)(2,1)} %bitcast.33), kind=kOutput, calls=%fused_computation.3 | convolution fusion | flops 537001984 | bytes 3407872 | tf_op jit(solution)/shard_map/jhst,jtf->hsf/dot_general | solution.py:33
  57.7 0.0 reduce-scatter.3.cloned.1.call-update
  57.7 0.0 all-gather.5.cloned.1.call-start
  57.7 0.0 copy-done.4
  57.8 10.0 %reduce-scatter.3.cloned.1.call-done = bf16[128,512]{1,0:T(8,128)(2,1)} async-done(((bf16[256,512]{1,0:T(8,128)(2,1)}), bf16[128,512]{1,0:T(8,128)(2,1)}) %reduce-scatter.3.cloned.1.call-update) | async-done | bytes 131088 | tf_op jit(solution)/shard_map/reduce_scatter | solution.py:41
  67.8 0.0 copy-done.3
  67.8 1.8 fusion.9
  69.6 0.0 copy-start.1
  69.6 0.0 all-gather.5.cloned.1.call-update
  69.6 0.0 reduce-scatter.5.cloned.1.call-start
  69.7 42.9 %all-gather.5.cloned.1.call-done = bf16[2048,512]{1,0:T(8,128)(2,1)} async-done(((bf16[128,512]{1,0:T(8,128)(2,1)}), bf16[2048,512]{1,0:T(8,128)(2,1)}) %all-gather.5.cloned.1.call-update) | async-done | bytes 2097168 | tf_op jit(solution)/shard_map/all_gather | solution.py:52
  112.6 3.0 %fusion.1 = bf16[256,512]{1,0:T(8,128)(2,1)} fusion(bf16[256,16,128]{2,0,1:T(8,128)(2,1)S(1)} %bitcast.30, bf16[16,128,512]{2,1,0:T(8,128)(2,1)} %bitcast.34), kind=kOutput, calls=%fused_computation.4 | convolution fusion | flops 537001984 | bytes 3407872 | tf_op jit(solution)/shard_map/jhst,jtf->hsf/dot_general | solution.py:33
  115.6 0.0 reduce-scatter.5.cloned.1.call-update
  115.6 0.0 all-reduce.2.cloned.1.call-start
  115.6 10.0 %reduce-scatter.5.cloned.1.call-done = bf16[128,512]{1,0:T(8,128)(2,1)} async-done(((bf16[256,512]{1,0:T(8,128)(2,1)}), bf16[128,512]{1,0:T(8,128)(2,1)}) %reduce-scatter.5.cloned.1.call-update) | async-done | bytes 131088 | tf_op jit(solution)/shard_map/reduce_scatter | solution.py:53
  125.7 0.0 copy-done.1
  125.7 0.0 copy-start.2
  125.7 2.3 convolution_bitcast_fusion
  127.9 0.0 all-reduce.2.cloned.1.call-update
  128.0 0.0 copy-done.2
  128.0 1.0 convolution_convert_fusion
  128.9 132.3 %all-reduce.2.cloned.1.call-done = f32[512,512]{0,1:T(8,128)} async-done(((f32[512,512]{0,1:T(8,128)}), f32[512,512]{0,1:T(8,128)}) %all-reduce.2.cloned.1.call-update) | async-done | bytes 1048592 | tf_op jit(solution)/shard_map/psum | solution.py:62
  261.2 2.5 copy.10
  (2 shorter events, 0.0 us)
Async XLA Ops:
  7.2 1.0 copy-start
  7.2 47.5 %all-gather.3.cloned.1.call-start = ((), (), s32[]{:S(2)}) async-start(), calls=%async_computation.2 | async-start | bytes 2228224 | tf_op jit(solution)/shard_map/all_gather | solution.py:40
  10.0 57.7 %reduce-scatter.3.cloned.1.call-start = ((), (), s32[]{:S(2)}) async-start(), calls=%async_computation.3 | async-start | bytes 393216 | tf_op jit(solution)/shard_map/reduce_scatter | solution.py:41
  12.3 45.5 %copy-start.4 = (s32[128]{0:T(128)S(1)}, s32[128]{0:T(128)}, u32[]{:S(2)}) copy-start(s32[128]{0:T(128)} %param.10) | copy-start | bytes 1540
  12.3 55.5 %copy-start.3 = (bf16[128,512]{1,0:T(8,128)(2,1)S(1)}, bf16[128,512]{1,0:T(8,128)(2,1)}, u32[]{:S(2)}) copy-start(bf16[128,512]{1,0:T(8,128)(2,1)} %param.11) | copy-start | bytes 393220
  57.7 54.9 %all-gather.5.cloned.1.call-start = ((), (), s32[]{:S(2)}) async-start(), calls=%async_computation.4 | async-start | bytes 2228224 | tf_op jit(solution)/shard_map/all_gather | solution.py:52
  69.6 56.1 %copy-start.1 = (bf16[128,512]{1,0:T(8,128)(2,1)S(1)}, bf16[128,512]{1,0:T(8,128)(2,1)}, u32[]{:S(2)}) copy-start(bf16[128,512]{1,0:T(8,128)(2,1)} %param.6) | copy-start | bytes 393220
  69.6 56.0 %reduce-scatter.5.cloned.1.call-start = ((), (), s32[]{:S(2)}) async-start(), calls=%async_computation.5 | async-start | bytes 393216 | tf_op jit(solution)/shard_map/reduce_scatter | solution.py:53
  115.6 145.6 %all-reduce.2.cloned.1.call-start = ((), (), s32[]{:S(2)}) async-start(), calls=%async_computation.6 | async-start | bytes 2097152 | tf_op jit(solution)/shard_map/psum | solution.py:62
  125.7 2.3 copy-start.2
Sparse Core Ops, SparseCore 0:
  10.7 43.9 all-gather.2
  57.8 9.9 reduce-scatter.2
  70.5 41.9 all-gather.4
  115.7 9.9 reduce-scatter.4
  131.3 129.9 all-reduce.1
where the time goes:
time: 272 us; the launch traced here: 270 us
  waiting for transfers between devices  238 us (88%)
  between operations  13.8 us (5%)
  matrix products  11 us (4%)
  other arithmetic  3.89 us (1%)
  local copies, waits for them, and re-layouts  3.64 us (1%)
    psum x1, waiting for transfers between devices, on_device(): weight_grad = lax.psum(local_term, ('rep', 'blk'))  132 us
    all_gather x1, waiting for transfers between devices, on_device(): folded = apply_tiles(lax.all_gather(grad_z, 'blk', axis=0, tiled=True))  42.9 us
    all_gather x1, waiting for transfers between devices, on_device(): lax.all_gather(projected, 'blk', axis=0, tiled=True)  42.4 us
    reduce_scatter x1, waiting for transfers between devices, on_device(): lax.psum_scatter(folded.reshape(2 * tile_rows, feat_width).astype(jnp.bfl...  10 us
    reduce_scatter x1, waiting for transfers between devices, on_device(): lax.psum_scatter(partial_value.reshape(2 * tile_rows, feat_width).astype(...  10 us
    dot_general x2, matrix products, apply_tiles(): jnp.einsum('jhst,jtf->hsf', masked, incoming.reshape(shard_count, tile_ro...  6 us
  transfers between devices with their start and end apart: 5, of which 5 were waited for; matrix products, arithmetic and copies ran while one was open for 1% of the time, Pallas kernels for 0%

commit v1 on v0

v1 whole, which is shorter than its diff:
```python
import functools
import math

import jax
import jax.numpy as jnp
from jax import lax
from jax.experimental import pallas as pl
from jax.experimental.pallas import tpu as pltpu
from jax.sharding import PartitionSpec as P

GELU_SCALE = math.sqrt(2.0 / math.pi)
CHUNKS = 2
MESH = pl.DeviceIdType.MESH


def activation(pre_act):
    inner = GELU_SCALE * (pre_act + 0.044715 * pre_act * pre_act * pre_act)
    tanh_part = jnp.tanh(inner)
    act_value = 0.5 * pre_act * (1.0 + tanh_part)
    act_slope = 0.5 * (1.0 + tanh_part) + 0.5 * pre_act * (
        1.0 - tanh_part * tanh_part
    ) * GELU_SCALE * (1.0 + 3.0 * 0.044715 * pre_act * pre_act)
    return (act_value, act_slope)


def kernel(
    n_blk, chunks,
    list_ref, mask_ref, x_ref, w_ref, tiles_ref, cot_ref,
    act_ref, wgrad_ref, fgrad_ref,
    xg, gg, wg, w_vm, tiles_vm, cot_vm, a2d, part, axs, axr, qs, qr,
    t_send, t_recv, wxs, wxr, ax_b, act_vm,
    local_sem, x_send, x_recv, g_send, g_recv, w_send, w_recv, wz_send,
    t_ssem, t_rsem, e_send, e_recv,
):
    nz = n_blk // 4
    rows = x_ref.shape[0]
    feat = x_ref.shape[1]
    fc = feat // chunks
    sl = feat // n_blk
    r = lax.axis_index("rep")
    me = lax.axis_index("blk")
    z = me // 4
    y = (me // 2) % 2
    core = me % 2

    def at(zz, yy, cc):
        return zz * 4 + yy * 2 + cc

    y_dev = at(z, 1 - y, core)
    p_dev = at(z, y, 1 - core)

    loads = [
        pltpu.make_async_copy(
            x_ref.at[:, pl.ds(c * fc, fc)], xg.at[c, me], local_sem.at[c]
        )
        for c in range(chunks)
    ]
    others = [
        pltpu.make_async_copy(tiles_ref, tiles_vm, local_sem.at[chunks]),
        pltpu.make_async_copy(w_ref, w_vm, local_sem.at[chunks + 1]),
        pltpu.make_async_copy(cot_ref, cot_vm, local_sem.at[chunks + 2]),
    ]
    for copy in loads + others:
        copy.start()

    barrier = pltpu.get_barrier_semaphore()
    for k in range(1, n_blk):
        pl.semaphore_signal(
            barrier, inc=1, device_id=(r, (me + k) % n_blk), device_id_type=MESH
        )
    pl.semaphore_signal(barrier, inc=1, device_id=(1 - r, me), device_id_type=MESH)
    for copy in loads:
        copy.wait()
    pl.semaphore_wait(barrier, n_blk)

    pending = []

    def send(cond, make):
        if cond is None:
            make().start()
        else:
            @pl.when(cond)
            def _():
                make().start()
        pending.append((cond, make))

    def block_copy(buf, ssem, rsem, slot, c, way, dev):
        def make():
            return pltpu.make_async_remote_copy(
                src_ref=buf(c, slot), dst_ref=buf(c, slot),
                send_sem=ssem.at[c, slot, way], recv_sem=rsem.at[c, slot],
                device_id=(r, dev), device_id_type=MESH,
            )
        return make

    def wait_block(buf, ssem, rsem, slot, c):
        pltpu.make_async_remote_copy(
            src_ref=buf(c, slot), dst_ref=buf(c, slot),
            send_sem=ssem.at[c, slot, 0], recv_sem=rsem.at[c, slot],
            device_id=(r, y_dev), device_id_type=MESH,
        ).wait_recv()

    def gather_own(buf, ssem, rsem, c):
        send(z < nz - 1, block_copy(buf, ssem, rsem, me, c, 0, at(z + 1, y, core)))
        send(z > 0, block_copy(buf, ssem, rsem, me, c, 1, at(z - 1, y, core)))
        send(None, block_copy(buf, ssem, rsem, me, c, 2, y_dev))
        send(None, block_copy(buf, ssem, rsem, me, c, 3, p_dev))

    def from_y(buf, ssem, rsem, zz, c, cond):
        slot = at(zz, 1 - y, core)
        go = block_copy(buf, ssem, rsem, slot, c, 3, p_dev)
        if cond is None:
            wait_block(buf, ssem, rsem, slot, c)
            go().start()
        else:
            @pl.when(cond)
            def _():
                wait_block(buf, ssem, rsem, slot, c)
                go().start()
        pending.append((cond, go))

    def from_z(buf, ssem, rsem, d, c, up):
        zz = z - d if up else z + d
        cond = (zz >= 0) if up else (zz < nz)
        slot = at(zz, y, core)
        nxt = z + 1 if up else z - 1
        more = (nxt < nz) if up else (nxt >= 0)
        go_z = block_copy(buf, ssem, rsem, slot, c, 0 if up else 1, at(nxt, y, core))
        go_y = block_copy(buf, ssem, rsem, slot, c, 2, y_dev)
        go_p = block_copy(buf, ssem, rsem, slot, c, 3, p_dev)

        @pl.when(cond)
        def _():
            wait_block(buf, ssem, rsem, slot, c)

            @pl.when(more)
            def _():
                go_z().start()

            go_y().start()
            go_p().start()

        pending.append((jnp.logical_and(cond, more), go_z))
        pending.append((cond, go_y))
        pending.append((cond, go_p))

    def gather_rest(buf, ssem, rsem):
        for d in range(1, nz):
            for c in range(chunks):
                from_z(buf, ssem, rsem, d, c, True)
                from_z(buf, ssem, rsem, d, c, False)
                if d == 1:
                    from_y(buf, ssem, rsem, z, c, None)
                else:
                    from_y(buf, ssem, rsem, z - d + 1, c, z - d + 1 >= 0)
                    from_y(buf, ssem, rsem, z + d - 1, c, z + d - 1 < nz)

    def gather_last(buf, ssem, rsem, c):
        d = nz
        if d == 1:
            from_y(buf, ssem, rsem, z, c, None)
        else:
            from_y(buf, ssem, rsem, z - d + 1, c, z - d + 1 >= 0)
            from_y(buf, ssem, rsem, z + d - 1, c, z + d - 1 < nz)
        for yy in range(2):
            for zz in range(nz):
                wait_block(buf, ssem, rsem, at(zz, yy, 1 - core), c)

    def exchange(src, dst, k):
        def make():
            return pltpu.make_async_remote_copy(
                src_ref=src, dst_ref=dst, send_sem=e_send.at[k], recv_sem=e_recv.at[k],
                device_id=(1 - r, me), device_id_type=MESH,
            )
        return make

    def xbuf(c, slot):
        return xg.at[c, slot]

    def gbuf(c, slot):
        return gg.at[c, slot]

    def wbuf(c, slot):
        return wg.at[slot, :, pl.ds(c * fc, fc)]

    for c in range(chunks):
        gather_own(xbuf, x_send, x_recv, c)

    others[0].wait()
    for j in range(n_blk):
        for h in range(2):
            here = jnp.logical_or(list_ref[2 * j] == h, list_ref[2 * j + 1] == h)
            keep = jnp.where(here, 1.0, 0.0).astype(jnp.float32)
            tile = tiles_vm[j, h * rows:(h + 1) * rows, :].astype(jnp.float32) * keep
            a2d[h * rows:(h + 1) * rows, j * rows:(j + 1) * rows] = tile.astype(jnp.bfloat16)

    gather_rest(xbuf, x_send, x_recv)
    ax_sends = []
    for c in range(chunks):
        gather_last(xbuf, x_send, x_recv, c)
        total = jnp.dot(
            a2d[:2 * rows, :], xg[c].reshape(n_blk * rows, fc),
            preferred_element_type=jnp.float32,
        )
        part[c] = total.reshape(2, rows, fc)
        axs[c] = part[c, 1 - r].astype(jnp.bfloat16)
        make = exchange(axs.at[c], axr.at[c], c)
        send(None, make)
        ax_sends.append(make)

    others[1].wait()
    others[2].wait()
    mask_cols = jnp.transpose(
        jnp.broadcast_to(mask_ref[...].astype(jnp.float32), (rows, rows))
    )
    for c in range(chunks):
        ax_sends[c]().wait_recv()
        ax = part[c, r] + axr[c].astype(jnp.float32)
        ax_b[:, c * fc:(c + 1) * fc] = ax.astype(jnp.bfloat16)
        slices = jnp.transpose(ax).reshape(fc // sl, sl, rows)
        t_send[c * (fc // sl):(c + 1) * (fc // sl)] = slices.astype(jnp.bfloat16)

    for c in range(chunks):
        summed = jnp.dot(
            ax_b[...], w_vm[:, c * fc:(c + 1) * fc], preferred_element_type=jnp.float32
        )
        act_value, act_slope = activation(summed)
        act_ref[:, c * fc:(c + 1) * fc] = act_value.astype(jnp.bfloat16)
        keep = jnp.concatenate([mask_cols] * (fc // rows), axis=1)
        cot = cot_vm[:, c * fc:(c + 1) * fc].astype(jnp.float32)
        gg[c, me] = (cot * keep * act_slope).astype(jnp.bfloat16)
        gather_own(gbuf, g_send, g_recv, c)

    t_copies = []
    for k in range(1, n_blk):
        peer = (me + k) % n_blk
        def t_make(peer=peer, k=k):
            return pltpu.make_async_remote_copy(
                src_ref=t_send.at[peer], dst_ref=t_recv.at[me],
                send_sem=t_ssem.at[k], recv_sem=t_rsem.at[k],
                device_id=(r, peer), device_id_type=MESH,
            )
        send(None, t_make)
        t_copies.append(t_make)
    t_recv[me] = t_send[me]

    gather_rest(gbuf, g_send, g_recv)
    for k in range(1, n_blk):
        origin = (me + n_blk - k) % n_blk
        pltpu.make_async_remote_copy(
            src_ref=t_send.at[origin], dst_ref=t_recv.at[origin],
            send_sem=t_ssem.at[k], recv_sem=t_rsem.at[k],
            device_id=(r, origin), device_id_type=MESH,
        ).wait_recv()
    for j in range(n_blk):
        a2d[2 * rows:2 * rows + sl, j * rows:(j + 1) * rows] = t_recv[j]

    q_makes, w_makes = [], []
    for c in range(chunks):
        gather_last(gbuf, g_send, g_recv, c)
        total = jnp.dot(
            a2d[...], gg[c].reshape(n_blk * rows, fc), preferred_element_type=jnp.float32
        )
        wxs[c] = total[2 * rows:, :].astype(jnp.bfloat16)
        make = exchange(wxs.at[c], wxr.at[c], chunks + c)
        send(None, make)
        w_makes.append(make)
        part[c] = total[:2 * rows, :].reshape(2, rows, fc)
        qs[c] = part[c, 1 - r].astype(jnp.bfloat16)
        make = exchange(qs.at[c], qr.at[c], 2 * chunks + c)
        send(None, make)
        q_makes.append(make)

    for c in range(chunks):
        w_makes[c]().wait_recv()
        both = wxs[c].astype(jnp.float32) + wxr[c].astype(jnp.float32)
        wg[me, :, c * fc:(c + 1) * fc] = both.astype(jnp.bfloat16)
        for zz in range(nz):
            def z_make(zz=zz, c=c):
                return pltpu.make_async_remote_copy(
                    src_ref=wbuf(c, me), dst_ref=wbuf(c, me),
                    send_sem=wz_send.at[c, zz], recv_sem=w_recv.at[c, me],
                    device_id=(r, at(zz, y, core)), device_id_type=MESH,
                )
            send(z != zz, z_make)
        send(None, block_copy(wbuf, w_send, w_recv, me, c, 0, y_dev))
        send(None, block_copy(wbuf, w_send, w_recv, me, c, 1, p_dev))

    fgrad = jnp.zeros((rows, feat), jnp.float32)
    for c in range(chunks):
        q_makes[c]().wait_recv()
        prop = (part[c, r] + qr[c].astype(jnp.float32)).astype(jnp.bfloat16)
        fgrad = fgrad + lax.dot_general(
            prop, w_vm[:, c * fc:(c + 1) * fc], (((1,), (1,)), ((), ())),
            preferred_element_type=jnp.float32,
        )
    fgrad_ref[...] = fgrad.astype(jnp.bfloat16)

    for c in range(chunks):
        for d in range(1, nz):
            for up in (True, False):
                zz = z - d if up else z + d
                cond = (zz >= 0) if up else (zz < nz)
                slot = at(zz, y, core)
                go_y = block_copy(wbuf, w_send, w_recv, slot, c, 0, y_dev)
                go_p = block_copy(wbuf, w_send, w_recv, slot, c, 1, p_dev)

                @pl.when(cond)
                def _():
                    wait_block(wbuf, w_send, w_recv, slot, c)
                    go_y().start()
                    go_p().start()

                pending.append((cond, go_y))
                pending.append((cond, go_p))
        for zz in range(nz):
            slot = at(zz, 1 - y, core)
            go_p = block_copy(wbuf, w_send, w_recv, slot, c, 1, p_dev)
            wait_block(wbuf, w_send, w_recv, slot, c)
            go_p().start()
            pending.append((None, go_p))
    for c in range(chunks):
        for yy in range(2):
            for zz in range(nz):
                wait_block(wbuf, w_send, w_recv, at(zz, yy, 1 - core), c)
    wgrad_ref[...] = wg[...]

    for cond, make in pending:
        if cond is None:
            make().wait_send()
        else:
            @pl.when(cond)
            def _():
                make().wait_send()


def on_device(features, weight, tile_values, tile_list, train_mask, cotangent, n_blk):
    rows, feat = features.shape
    chunks = CHUNKS
    fc = feat // chunks
    sl = feat // n_blk
    bf = jnp.bfloat16
    vm = pltpu.VMEM
    dma = pltpu.SemaphoreType.DMA
    any_spec = pl.BlockSpec(memory_space=pl.ANY)
    vmem_spec = pl.BlockSpec(memory_space=pltpu.VMEM)
    act, wgrad, fgrad = pl.pallas_call(
        functools.partial(kernel, n_blk, chunks),
        out_shape=(
            jax.ShapeDtypeStruct((rows, feat), bf),
            jax.ShapeDtypeStruct((n_blk, sl, feat), bf),
            jax.ShapeDtypeStruct((rows, feat), bf),
        ),
        in_specs=[
            pl.BlockSpec(memory_space=pltpu.SMEM), vmem_spec,
            any_spec, any_spec, any_spec, any_spec,
        ],
        out_specs=(vmem_spec, vmem_spec, vmem_spec),
        scratch_shapes=[
            vm((chunks, n_blk, rows, fc), bf),
            vm((chunks, n_blk, rows, fc), bf),
            vm((n_blk, sl, feat), bf),
            vm((feat, feat), bf),
            vm((n_blk, 2 * rows, rows), bf),
            vm((rows, feat), bf),
            vm((2 * rows + sl, n_blk * rows), bf),
            vm((chunks, 2, rows, fc), jnp.float32),
            vm((chunks, rows, fc), bf),
            vm((chunks, rows, fc), bf),
            vm((chunks, rows, fc), bf),
            vm((chunks, rows, fc), bf),
            vm((n_blk, sl, rows), bf),
            vm((n_blk, sl, rows), bf),
            vm((chunks, sl, fc), bf),
            vm((chunks, sl, fc), bf),
            vm((rows, feat), bf),
            vm((8, 128), bf),
            dma((chunks + 3,)),
            dma((chunks, n_blk, 4)), dma((chunks, n_blk)),
            dma((chunks, n_blk, 4)), dma((chunks, n_blk)),
            dma((chunks, n_blk, 2)), dma((chunks, n_blk)),
            dma((chunks, n_blk // 4)),
            dma((n_blk,)), dma((n_blk,)),
            dma((3 * chunks,)), dma((3 * chunks,)),
        ],
        compiler_params=pltpu.CompilerParams(
            collective_id=0, has_side_effects=True, vmem_limit_bytes=56 * 1024 * 1024
        ),
    )(
        tile_list.reshape(-1), train_mask.reshape(1, rows), features, weight,
        tile_values.reshape(n_blk, 2 * rows, rows), cotangent,
    )
    return act, wgrad.reshape(feat, feat).astype(jnp.float32), fgrad


def solution(mesh):
    in_specs = (
        P(("rep", "blk"), None),
        P(),
        P("rep", "blk", None, None, None, None),
        P("rep", "blk", None, None),
        P(("rep", "blk")),
        P(("rep", "blk"), None),
    )
    out_specs = (P(("rep", "blk"), None), P(), P(("rep", "blk"), None))
    body = functools.partial(on_device, n_blk=mesh.shape["blk"])
    return jax.shard_map(
        body, mesh=mesh, in_specs=in_specs, out_specs=out_specs, check_vma=False
    )
```

time: 272 us -> 68 us (0.25)
  waiting for transfers between devices: 238 us -> 0 us
  Pallas kernels: 0 us -> 62 us
  between operations: 13.8 us -> 0.66 us
  matrix products: 11 us -> 0 us
    psum x1 -> x0, waiting for transfers between devices: 132 us -> none  [on_device(): weight_grad = lax.psum(local_term, ('rep', 'blk'))]
    all_gather x2 -> x0, waiting for transfers between devices: 85.3 us -> none  [the longest x1 42.9 us: on_device(): folded = apply_tiles(lax.all_gather(grad_z, 'blk', axis=0, tiled=True))]
    pallas_call x0 -> x1, Pallas kernels: none -> 62 us  [on_device(): pl.pallas_call(functools.partial(kernel, n_blk, chunks), out_shape=(jax.S...]
    reduce_scatter x2 -> x0, waiting for transfers between devices: 20 us -> none  [the longest x1 10 us: on_device(): lax.psum_scatter(folded.reshape(2 * tile_rows, feat_width).astype(jnp.bfl...]
    dot_general x5 -> x0, matrix products: 11 us -> none  [the longest x2 6 us: apply_tiles(): jnp.einsum('jhst,jtf->hsf', masked, incoming.reshape(shard_count, tile_ro...]
  transfers between devices with their start and end apart: 5 -> 0, of which waited for: 5 -> 0; matrix products, arithmetic and copies ran while one was open for 1% -> 0% of each run, Pallas kernels for 0% -> 0%
where the time goes in v1:
time: 68 us; the launch traced here: 67.8 us
  Pallas kernels  62 us (91%)
  local copies, waits for them, and re-layouts  2.97 us (4%)
  other arithmetic  2.18 us (3%)
    pallas_call x1, Pallas kernels, on_device(): pl.pallas_call(functools.partial(kernel, n_blk, chunks), out_shape=(jax.S...  62 us
    unnamed x9, local copies, waits for them, and re-layouts  2.36 us
    convert_element_type x1, other arithmetic, on_device(): return (act, wgrad.reshape(feat, feat).astype(jnp.float32), fgrad)  2.18 us

profile of v1, /device:TPU:1, one launch (start us, length us, event | category | flops | bytes accessed | tf_op | source)
XLA Modules:
  0.0 67.8 jit_solution(12692660792859236470)
XLA Ops:
  0.6 0.0 copy-start.2
  0.6 0.7 copy-done.2
  1.3 0.1 copy.10
  1.4 0.6 reshape.18.list_ref
  2.0 62.0 %shard_map.85 = (bf16[128,512]{1,0:T(8,128)(2,1)}, bf16[16,32,512]{2,1,0:T(8,128)(2,1)}, bf16[128,512]{1,0:T(8,128)(2,1)}) custom-call(s32[32]{0:T(128)} %reshape.18.list_ref, s32[1,128]{1,0:T(1,128)} %bitcast.8, bf16[128,512]{1,0:T(8,128)(2,1)} %x_ref.1, bf16[512,512]{1,0:T(8,128)(2,1)} %w_ref.1, bf16[16,256,128]{2,1,0:T(8,128)(2,1)} %bitcast.7, ...), custom_call_target="tpu_custom_call" | custom-call | tf_op jit(solution)/shard_map/pallas_call | solution.py:347
  64.0 0.0 copy-start.1
  64.1 2.2 %bitcast_convert_fusion = f32[512,512]{1,0:T(8,128)} fusion(bf16[16,32,512]{2,1,0:T(8,128)(2,1)} %get-tuple-element.7), kind=kLoop, calls=%fused_computation | loop fusion | flops 262144 | bytes 1572864 | tf_op jit(solution)/shard_map/convert_element_type | solution.py:393
  66.2 0.0 copy-done.1
  66.2 0.0 copy-start
  66.2 0.7 copy.13
  66.9 0.3 copy-done
  67.2 0.7 copy.14
Async XLA Ops:
  0.6 0.7 %copy-start.2 = (s32[1,1,16,2]{2,3,1,0:T(2,128)S(1)}, s32[1,1,16,2]{2,3,1,0:T(2,128)}, u32[]{:S(2)}) copy-start(s32[1,1,16,2]{2,3,1,0:T(2,128)} %param.9) | copy-start | bytes 388
  64.0 2.2 %copy-start.1 = (bf16[128,512]{1,0:T(8,128)(2,1)S(1)}, bf16[128,512]{1,0:T(8,128)(2,1)}, u32[]{:S(2)}) copy-start(bf16[128,512]{1,0:T(8,128)(2,1)} %get-tuple-element.12) | copy-start | bytes 393220
  66.2 1.0 %copy-start = (bf16[128,512]{1,0:T(8,128)(2,1)S(1)}, bf16[128,512]{1,0:T(8,128)(2,1)}, u32[]{:S(2)}) copy-start(bf16[128,512]{1,0:T(8,128)(2,1)} %get-tuple-element.14) | copy-start | bytes 393220

commit v2 on v1

--- a/solution.py
+++ b/solution.py
@@ -10,6 +10,12 @@
 
 GELU_SCALE = math.sqrt(2.0 / math.pi)
 CHUNKS = 2
+X_CHUNKS = 2
+G_CHUNKS = 2
+W_CHUNKS = 1
+T_EARLY = 0
+NEAR = 1
+FIN = 1
 MESH = pl.DeviceIdType.MESH
 
 
@@ -24,7 +30,7 @@
 
 
 def kernel(
-    n_blk, chunks,
+    n_blk, chunks, xc, gc, wc,
     list_ref, mask_ref, x_ref, w_ref, tiles_ref, cot_ref,
     act_ref, wgrad_ref, fgrad_ref,
     xg, gg, wg, w_vm, tiles_vm, cot_vm, a2d, part, axs, axr, qs, qr,
@@ -50,28 +56,37 @@
     p_dev = at(z, y, 1 - core)
 
     loads = [
-        pltpu.make_async_copy(
-            x_ref.at[:, pl.ds(c * fc, fc)], xg.at[c, me], local_sem.at[c]
-        )
-        for c in range(chunks)
+        pltpu.make_async_copy(x_ref, xg.at[me], local_sem.at[3])
     ]
     others = [
-        pltpu.make_async_copy(tiles_ref, tiles_vm, local_sem.at[chunks]),
-        pltpu.make_async_copy(w_ref, w_vm, local_sem.at[chunks + 1]),
-        pltpu.make_async_copy(cot_ref, cot_vm, local_sem.at[chunks + 2]),
+        pltpu.make_async_copy(tiles_ref, tiles_vm, local_sem.at[0]),
+        pltpu.make_async_copy(w_ref, w_vm, local_sem.at[1]),
+        pltpu.make_async_copy(cot_ref, cot_vm, local_sem.at[2]),
     ]
     for copy in loads + others:
         copy.start()
 
     barrier = pltpu.get_barrier_semaphore()
-    for k in range(1, n_blk):
-        pl.semaphore_signal(
-            barrier, inc=1, device_id=(r, (me + k) % n_blk), device_id_type=MESH
-        )
+    if NEAR:
+        near = [(None, y_dev), (None, p_dev), (z > 0, at(z - 1, y, core)),
+                (z < nz - 1, at(z + 1, y, core))]
+    else:
+        near = [(None, (me + k) % n_blk) for k in range(1, n_blk)]
+    for cond, dev in near:
+        def greet(dev=dev):
+            pl.semaphore_signal(barrier, inc=1, device_id=(r, dev), device_id_type=MESH)
+        if cond is None:
+            greet()
+        else:
+            pl.when(cond)(greet)
     pl.semaphore_signal(barrier, inc=1, device_id=(1 - r, me), device_id_type=MESH)
     for copy in loads:
         copy.wait()
-    pl.semaphore_wait(barrier, n_blk)
+    if NEAR:
+        ends = (z == 0).astype(jnp.int32) + (z == nz - 1).astype(jnp.int32)
+        pl.semaphore_wait(barrier, 5 - ends)
+    else:
+        pl.semaphore_wait(barrier, n_blk)
 
     pending = []
 
@@ -144,7 +159,7 @@
         pending.append((cond, go_y))
         pending.append((cond, go_p))
 
-    def gather_rest(buf, ssem, rsem):
+    def gather_rest(buf, ssem, rsem, chunks):
         for d in range(1, nz):
             for c in range(chunks):
                 from_z(buf, ssem, rsem, d, c, True)
@@ -175,31 +190,32 @@
         return make
 
     def xbuf(c, slot):
-        return xg.at[c, slot]
+        return xg.at[slot, :, pl.ds(c * (feat // xc), feat // xc)]
 
     def gbuf(c, slot):
-        return gg.at[c, slot]
+        return gg.at[slot, :, pl.ds(c * (feat // gc), feat // gc)]
 
     def wbuf(c, slot):
-        return wg.at[slot, :, pl.ds(c * fc, fc)]
-
-    for c in range(chunks):
+        return wg.at[slot, :, pl.ds(c * (feat // wc), feat // wc)]
+
+    for c in range(xc):
         gather_own(xbuf, x_send, x_recv, c)
 
     others[0].wait()
     for j in range(n_blk):
         for h in range(2):
-            here = jnp.logical_or(list_ref[2 * j] == h, list_ref[2 * j + 1] == h)
+            here = jnp.logical_or(list_ref[0, j] == h, list_ref[1, j] == h)
             keep = jnp.where(here, 1.0, 0.0).astype(jnp.float32)
             tile = tiles_vm[j, h * rows:(h + 1) * rows, :].astype(jnp.float32) * keep
             a2d[h * rows:(h + 1) * rows, j * rows:(j + 1) * rows] = tile.astype(jnp.bfloat16)
 
-    gather_rest(xbuf, x_send, x_recv)
+    gather_rest(xbuf, x_send, x_recv, xc)
     ax_sends = []
     for c in range(chunks):
-        gather_last(xbuf, x_send, x_recv, c)
+        if c < xc:
+            gather_last(xbuf, x_send, x_recv, c)
         total = jnp.dot(
-            a2d[:2 * rows, :], xg[c].reshape(n_blk * rows, fc),
+            a2d[:2 * rows, :], xg[:, :, c * fc:(c + 1) * fc].reshape(n_blk * rows, fc),
             preferred_element_type=jnp.float32,
         )
         part[c] = total.reshape(2, rows, fc)
@@ -220,6 +236,23 @@
         slices = jnp.transpose(ax).reshape(fc // sl, sl, rows)
         t_send[c * (fc // sl):(c + 1) * (fc // sl)] = slices.astype(jnp.bfloat16)
 
+    def send_slices():
+        t_copies = []
+        for k in range(1, n_blk):
+            peer = (me + k) % n_blk
+            def t_make(peer=peer, k=k):
+                return pltpu.make_async_remote_copy(
+                    src_ref=t_send.at[peer], dst_ref=t_recv.at[me],
+                    send_sem=t_ssem.at[k], recv_sem=t_rsem.at[k],
+                    device_id=(r, peer), device_id_type=MESH,
+                )
+            send(None, t_make)
+            t_copies.append(t_make)
+        t_recv[me] = t_send[me]
+
+    if T_EARLY:
+        send_slices()
+
     for c in range(chunks):
         summed = jnp.dot(
             ax_b[...], w_vm[:, c * fc:(c + 1) * fc], preferred_element_type=jnp.float32
@@ -228,23 +261,16 @@
         act_ref[:, c * fc:(c + 1) * fc] = act_value.astype(jnp.bfloat16)
         keep = jnp.concatenate([mask_cols] * (fc // rows), axis=1)
         cot = cot_vm[:, c * fc:(c + 1) * fc].astype(jnp.float32)
-        gg[c, me] = (cot * keep * act_slope).astype(jnp.bfloat16)
-        gather_own(gbuf, g_send, g_recv, c)
-
-    t_copies = []
-    for k in range(1, n_blk):
-        peer = (me + k) % n_blk
-        def t_make(peer=peer, k=k):
-            return pltpu.make_async_remote_copy(
-                src_ref=t_send.at[peer], dst_ref=t_recv.at[me],
-                send_sem=t_ssem.at[k], recv_sem=t_rsem.at[k],
-                device_id=(r, peer), device_id_type=MESH,
-            )
-        send(None, t_make)
-        t_copies.append(t_make)
-    t_recv[me] = t_send[me]
-
-    gather_rest(gbuf, g_send, g_recv)
+        gg[me, :, c * fc:(c + 1) * fc] = (cot * keep * act_slope).astype(jnp.bfloat16)
+        if gc == chunks:
+            gather_own(gbuf, g_send, g_recv, c)
+    if gc == 1:
+        gather_own(gbuf, g_send, g_recv, 0)
+
+    if not T_EARLY:
+        send_slices()
+
+    gather_rest(gbuf, g_send, g_recv, gc)
     for k in range(1, n_blk):
         origin = (me + n_blk - k) % n_blk
         pltpu.make_async_remote_copy(
@@ -257,24 +283,33 @@
 
     q_makes, w_makes = [], []
     for c in range(chunks):
-        gather_last(gbuf, g_send, g_recv, c)
+        if c < gc:
+            gather_last(gbuf, g_send, g_recv, c)
         total = jnp.dot(
-            a2d[...], gg[c].reshape(n_blk * rows, fc), preferred_element_type=jnp.float32
+            a2d[...], gg[:, :, c * fc:(c + 1) * fc].reshape(n_blk * rows, fc), preferred_element_type=jnp.float32
         )
-        wxs[c] = total[2 * rows:, :].astype(jnp.bfloat16)
-        make = exchange(wxs.at[c], wxr.at[c], chunks + c)
-        send(None, make)
-        w_makes.append(make)
+        wxs[:, c * fc:(c + 1) * fc] = total[2 * rows:, :].astype(jnp.bfloat16)
+        if wc == chunks:
+            cols = pl.ds(c * fc, fc)
+            make = exchange(wxs.at[:, cols], wxr.at[:, cols], chunks + c)
+            send(None, make)
+            w_makes.append(make)
+        elif c == chunks - 1:
+            make = exchange(wxs, wxr, chunks)
+            send(None, make)
+            w_makes.append(make)
         part[c] = total[:2 * rows, :].reshape(2, rows, fc)
         qs[c] = part[c, 1 - r].astype(jnp.bfloat16)
         make = exchange(qs.at[c], qr.at[c], 2 * chunks + c)
         send(None, make)
         q_makes.append(make)
 
-    for c in range(chunks):
+    wf = feat // wc
+    for c in range(wc):
         w_makes[c]().wait_recv()
-        both = wxs[c].astype(jnp.float32) + wxr[c].astype(jnp.float32)
-        wg[me, :, c * fc:(c + 1) * fc] = both.astype(jnp.bfloat16)
+        cols = slice(c * wf, (c + 1) * wf)
+        both = wxs[:, cols].astype(jnp.float32) + wxr[:, cols].astype(jnp.float32)
+        wg[me, :, cols] = both.astype(jnp.bfloat16)
         for zz in range(nz):
             def z_make(zz=zz, c=c):
                 return pltpu.make_async_remote_copy(
@@ -296,7 +331,7 @@
         )
     fgrad_ref[...] = fgrad.astype(jnp.bfloat16)
 
-    for c in range(chunks):
+    for c in range(wc):
         for d in range(1, nz):
             for up in (True, False):
                 zz = z - d if up else z + d
@@ -319,7 +354,7 @@
             wait_block(wbuf, w_send, w_recv, slot, c)
             go_p().start()
             pending.append((None, go_p))
-    for c in range(chunks):
+    for c in range(wc):
         for yy in range(2):
             for zz in range(nz):
                 wait_block(wbuf, w_send, w_recv, at(zz, yy, 1 - core), c)
@@ -332,6 +367,27 @@
             @pl.when(cond)
             def _():
                 make().wait_send()
+
+
+def widen(act_in, w_in, f_in, act_out, w_out, f_out, act_vm, w_vm, f_vm, wide_vm, in_sem, out_sem):
+    ins = [
+        pltpu.make_async_copy(src, dst, in_sem.at[i])
+        for i, (src, dst) in enumerate(((w_in, w_vm), (act_in, act_vm), (f_in, f_vm)))
+    ]
+    outs = [
+        pltpu.make_async_copy(src, dst, out_sem.at[i])
+        for i, (src, dst) in enumerate(((wide_vm, w_out), (act_vm, act_out), (f_vm, f_out)))
+    ]
+    for copy in ins:
+        copy.start()
+    ins[0].wait()
+    wide_vm[...] = w_vm[...].astype(jnp.float32)
+    outs[0].start()
+    for i in (1, 2):
+        ins[i].wait()
+        outs[i].start()
+    for copy in outs:
+        copy.wait()
 
 
 def on_device(features, weight, tile_values, tile_list, train_mask, cotangent, n_blk):
@@ -345,7 +401,7 @@
     any_spec = pl.BlockSpec(memory_space=pl.ANY)
     vmem_spec = pl.BlockSpec(memory_space=pltpu.VMEM)
     act, wgrad, fgrad = pl.pallas_call(
-        functools.partial(kernel, n_blk, chunks),
+        functools.partial(kernel, n_blk, chunks, X_CHUNKS, G_CHUNKS, W_CHUNKS),
         out_shape=(
             jax.ShapeDtypeStruct((rows, feat), bf),
             jax.ShapeDtypeStruct((n_blk, sl, feat), bf),
@@ -357,8 +413,8 @@
         ],
         out_specs=(vmem_spec, vmem_spec, vmem_spec),
         scratch_shapes=[
-            vm((chunks, n_blk, rows, fc), bf),
-            vm((chunks, n_blk, rows, fc), bf),
+            vm((n_blk, rows, feat), bf),
+            vm((n_blk, rows, feat), bf),
             vm((n_blk, sl, feat), bf),
             vm((feat, feat), bf),
             vm((n_blk, 2 * rows, rows), bf),
@@ -371,11 +427,11 @@
             vm((chunks, rows, fc), bf),
             vm((n_blk, sl, rows), bf),
             vm((n_blk, sl, rows), bf),
-            vm((chunks, sl, fc), bf),
-            vm((chunks, sl, fc), bf),
+            vm((sl, feat), bf),
+            vm((sl, feat), bf),
             vm((rows, feat), bf),
             vm((8, 128), bf),
-            dma((chunks + 3,)),
+            dma((4,)),
             dma((chunks, n_blk, 4)), dma((chunks, n_blk)),
             dma((chunks, n_blk, 4)), dma((chunks, n_blk)),
             dma((chunks, n_blk, 2)), dma((chunks, n_blk)),
@@ -387,10 +443,25 @@
             collective_id=0, has_side_effects=True, vmem_limit_bytes=56 * 1024 * 1024
         ),
     )(
-        tile_list.reshape(-1), train_mask.reshape(1, rows), features, weight,
+        jnp.transpose(tile_list[0, 0]), train_mask.reshape(1, rows), features, weight,
         tile_values.reshape(n_blk, 2 * rows, rows), cotangent,
     )
-    return act, wgrad.reshape(feat, feat).astype(jnp.float32), fgrad
+    if not FIN:
+        return act, wgrad.reshape(feat, feat).astype(jnp.float32), fgrad
+    return pl.pallas_call(
+        widen,
+        out_shape=(
+            jax.ShapeDtypeStruct((rows, feat), bf),
+            jax.ShapeDtypeStruct((feat, feat), jnp.float32),
+            jax.ShapeDtypeStruct((rows, feat), bf),
+        ),
+        in_specs=[any_spec] * 3,
+        out_specs=(any_spec,) * 3,
+        scratch_shapes=[
+            vm((rows, feat), bf), vm((feat, feat), bf), vm((rows, feat), bf),
+            vm((feat, feat), jnp.float32), dma((3,)), dma((3,)),
+        ],
+    )(act, wgrad.reshape(feat, feat), fgrad)
 
 
 def solution(mesh):

time: 68 us -> 62.1 us (0.913)
  local copies, waits for them, and re-layouts: 2.97 us -> 0 us
  other arithmetic: 2.18 us -> 0 us
  Pallas kernels: 62 us -> 61.3 us
    unnamed x9 -> x0, local copies, waits for them, and re-layouts: 2.36 us -> none
    convert_element_type x1 -> x0, other arithmetic: 2.18 us -> none  [on_device(): return (act, wgrad.reshape(feat, feat).astype(jnp.float32), fgrad)]
    pallas_call x1 -> x2, Pallas kernels: 62 us -> 61.3 us  [the longest x1 59.1 us: on_device(): pl.pallas_call(functools.partial(kernel, n_blk, chunks, X_CHUNKS, G_CHUNK...]
where the time goes in v2:
time: 62.1 us; the launch traced here: 61.9 us
  Pallas kernels  61.3 us (99%)
  between operations  0.64 us (1%)
    pallas_call x1, Pallas kernels, on_device(): pl.pallas_call(functools.partial(kernel, n_blk, chunks, X_CHUNKS, G_CHUNK...  59.1 us
    pallas_call x1, Pallas kernels, on_device(): pl.pallas_call(widen, out_shape=(jax.ShapeDtypeStruct((rows, feat), bf),...  2.21 us

profile of v2, /device:TPU:1, one launch (start us, length us, event | category | flops | bytes accessed | tf_op | source)
XLA Modules:
  0.0 61.9 jit_solution(13710314772689652523)
XLA Ops:
  0.6 59.1 %shard_map.85 = (bf16[128,512]{1,0:T(8,128)(2,1)}, bf16[16,32,512]{2,1,0:T(8,128)(2,1)}, bf16[128,512]{1,0:T(8,128)(2,1)}) custom-call(s32[2,16]{1,0:T(2,128)} %bitcast.8, s32[1,128]{1,0:T(1,128)} %bitcast.9, bf16[128,512]{1,0:T(8,128)(2,1)} %x_ref.1, bf16[512,512]{1,0:T(8,128)(2,1)} %w_ref.1, bf16[16,256,128]{2,1,0:T(8,128)(2,1)} %bitcast.6, ...), custom_call_target="tpu_custom_call" | custom-call | tf_op jit(solution)/shard_map/pallas_call | solution.py:403
  59.7 2.2 %shard_map.86 = (bf16[128,512]{1,0:T(8,128)(2,1)}, f32[512,512]{1,0:T(8,128)}, bf16[128,512]{1,0:T(8,128)(2,1)}) custom-call(bf16[128,512]{1,0:T(8,128)(2,1)} %get-tuple-element.6.act_in, bf16[512,512]{1,0:T(8,128)(2,1)} %bitcast.7, bf16[128,512]{1,0:T(8,128)(2,1)} %get-tuple-element.8.f_in), custom_call_target="tpu_custom_call" | custom-call | tf_op jit(solution)/shard_map/pallas_call | solution.py:451

commit v3 on v2

--- a/solution.py
+++ b/solution.py
@@ -34,7 +34,7 @@
     list_ref, mask_ref, x_ref, w_ref, tiles_ref, cot_ref,
     act_ref, wgrad_ref, fgrad_ref,
     xg, gg, wg, w_vm, tiles_vm, cot_vm, a2d, part, axs, axr, qs, qr,
-    t_send, t_recv, wxs, wxr, ax_b, act_vm,
+    t_send, t_recv, wxs, wxr, ax_b, act_vm, fgrad_vm,
     local_sem, x_send, x_recv, g_send, g_recv, w_send, w_recv, wz_send,
     t_ssem, t_rsem, e_send, e_recv,
 ):
@@ -209,6 +209,11 @@
             tile = tiles_vm[j, h * rows:(h + 1) * rows, :].astype(jnp.float32) * keep
             a2d[h * rows:(h + 1) * rows, j * rows:(j + 1) * rows] = tile.astype(jnp.bfloat16)
 
+    others[1].wait()
+    others[2].wait()
+    mask_cols = jnp.transpose(
+        jnp.broadcast_to(mask_ref[...].astype(jnp.float32), (rows, rows))
+    )
     gather_rest(xbuf, x_send, x_recv, xc)
     ax_sends = []
     for c in range(chunks):
@@ -224,19 +229,16 @@
         send(None, make)
         ax_sends.append(make)
 
-    others[1].wait()
-    others[2].wait()
-    mask_cols = jnp.transpose(
-        jnp.broadcast_to(mask_ref[...].astype(jnp.float32), (rows, rows))
-    )
     for c in range(chunks):
         ax_sends[c]().wait_recv()
         ax = part[c, r] + axr[c].astype(jnp.float32)
         ax_b[:, c * fc:(c + 1) * fc] = ax.astype(jnp.bfloat16)
-        slices = jnp.transpose(ax).reshape(fc // sl, sl, rows)
-        t_send[c * (fc // sl):(c + 1) * (fc // sl)] = slices.astype(jnp.bfloat16)
 
     def send_slices():
+        for c in range(chunks):
+            ax = ax_b[:, c * fc:(c + 1) * fc].astype(jnp.float32)
+            slices = jnp.transpose(ax).reshape(fc // sl, sl, rows)
+            t_send[c * (fc // sl):(c + 1) * (fc // sl)] = slices.astype(jnp.bfloat16)
         t_copies = []
         for k in range(1, n_blk):
             peer = (me + k) % n_blk
@@ -258,7 +260,7 @@
             ax_b[...], w_vm[:, c * fc:(c + 1) * fc], preferred_element_type=jnp.float32
         )
         act_value, act_slope = activation(summed)
-        act_ref[:, c * fc:(c + 1) * fc] = act_value.astype(jnp.bfloat16)
+        act_vm[:, c * fc:(c + 1) * fc] = act_value.astype(jnp.bfloat16)
         keep = jnp.concatenate([mask_cols] * (fc // rows), axis=1)
         cot = cot_vm[:, c * fc:(c + 1) * fc].astype(jnp.float32)
         gg[me, :, c * fc:(c + 1) * fc] = (cot * keep * act_slope).astype(jnp.bfloat16)
@@ -269,6 +271,8 @@
 
     if not T_EARLY:
         send_slices()
+    act_out = pltpu.make_async_copy(act_vm, act_ref, local_sem.at[0])
+    act_out.start()
 
     gather_rest(gbuf, g_send, g_recv, gc)
     for k in range(1, n_blk):
@@ -329,7 +333,9 @@
             prop, w_vm[:, c * fc:(c + 1) * fc], (((1,), (1,)), ((), ())),
             preferred_element_type=jnp.float32,
         )
-    fgrad_ref[...] = fgrad.astype(jnp.bfloat16)
+    fgrad_vm[...] = fgrad.astype(jnp.bfloat16)
+    fgrad_out = pltpu.make_async_copy(fgrad_vm, fgrad_ref, local_sem.at[1])
+    fgrad_out.start()
 
     for c in range(wc):
         for d in range(1, nz):
@@ -358,7 +364,8 @@
         for yy in range(2):
             for zz in range(nz):
                 wait_block(wbuf, w_send, w_recv, at(zz, yy, 1 - core), c)
-    wgrad_ref[...] = wg[...]
+    w_out = pltpu.make_async_copy(wg, wgrad_ref, local_sem.at[2])
+    w_out.start()
 
     for cond, make in pending:
         if cond is None:
@@ -367,6 +374,10 @@
             @pl.when(cond)
             def _():
                 make().wait_send()
+
+    act_out.wait()
+    fgrad_out.wait()
+    w_out.wait()
 
 
 def widen(act_in, w_in, f_in, act_out, w_out, f_out, act_vm, w_vm, f_vm, wide_vm, in_sem, out_sem):
@@ -411,7 +422,7 @@
             pl.BlockSpec(memory_space=pltpu.SMEM), vmem_spec,
             any_spec, any_spec, any_spec, any_spec,
         ],
-        out_specs=(vmem_spec, vmem_spec, vmem_spec),
+        out_specs=(any_spec, any_spec, any_spec),
         scratch_shapes=[
             vm((n_blk, rows, feat), bf),
             vm((n_blk, rows, feat), bf),
@@ -430,7 +441,8 @@
             vm((sl, feat), bf),
             vm((sl, feat), bf),
             vm((rows, feat), bf),
-            vm((8, 128), bf),
+            vm((rows, feat), bf),
+            vm((rows, feat), bf),
             dma((4,)),
             dma((chunks, n_blk, 4)), dma((chunks, n_blk)),
             dma((chunks, n_blk, 4)), dma((chunks, n_blk)),

time: 62.1 us -> 61.7 us (level)
  no operation moved by 1% of the time
where the time goes in v3:
time: 61.7 us; the launch traced here: 61.6 us
  Pallas kernels  60.9 us (99%)
  between operations  0.64 us (1%)
    pallas_call x1, Pallas kernels, on_device(): pl.pallas_call(functools.partial(kernel, n_blk, chunks, X_CHUNKS, G_CHUNK...  58.7 us
    pallas_call x1, Pallas kernels, on_device(): pl.pallas_call(widen, out_shape=(jax.ShapeDtypeStruct((rows, feat), bf),...  2.21 us

profile of v3, /device:TPU:1, one launch (start us, length us, event | category | flops | bytes accessed | tf_op | source)
XLA Modules:
  0.0 61.6 jit_solution(17811936680157147222)
XLA Ops:
  0.6 58.7 %shard_map.85 = (bf16[128,512]{1,0:T(8,128)(2,1)}, bf16[16,32,512]{2,1,0:T(8,128)(2,1)}, bf16[128,512]{1,0:T(8,128)(2,1)}) custom-call(s32[2,16]{1,0:T(2,128)} %bitcast.8, s32[1,128]{1,0:T(1,128)} %bitcast.9, bf16[128,512]{1,0:T(8,128)(2,1)} %x_ref.1, bf16[512,512]{1,0:T(8,128)(2,1)} %w_ref.1, bf16[16,256,128]{2,1,0:T(8,128)(2,1)} %bitcast.6, ...), custom_call_target="tpu_custom_call" | custom-call | tf_op jit(solution)/shard_map/pallas_call | solution.py:414
  59.4 2.2 %shard_map.86 = (bf16[128,512]{1,0:T(8,128)(2,1)}, f32[512,512]{1,0:T(8,128)}, bf16[128,512]{1,0:T(8,128)(2,1)}) custom-call(bf16[128,512]{1,0:T(8,128)(2,1)} %get-tuple-element.6.act_in, bf16[512,512]{1,0:T(8,128)(2,1)} %bitcast.7, bf16[128,512]{1,0:T(8,128)(2,1)} %get-tuple-element.8.f_in), custom_call_target="tpu_custom_call" | custom-call | tf_op jit(solution)/shard_map/pallas_call | solution.py:463
